TPU v7x, 32 devices: a whole 2x2x4 slice. The times are simulated.
32 devices in a mesh: section: 4 (over y, x), tensor: 8 (over z, core).
Axes of the slice: x: 2, y: 2, z: 4, core: 2. Of those that a mesh axis runs over, the one named last changes fastest.
Arguments:
- hidden_last: bfloat16 [512, 6656], P(None, 'tensor'), may hold values from -6 to 6
- labels: int32 [512], replicated, may hold values from 0 to 31999
- head_weight: bfloat16 [6656, 32000], P(None, 'tensor'), may hold values from -0.21875 to 0.21875
- layer_inputs: bfloat16 [4, 512, 6656], P('section', None, 'tensor'), may hold values from -6 to 6
- weights: bfloat16 [4, 6656, 6656], P('section', 'tensor'), may hold values from -0.078125 to 0.078125
- row_state: float32 [4, 6656], P('section', 'tensor'), may hold values from 1.173753e-06 to 0.000498845
- col_state: float32 [4, 6656], P('section'), may hold values from 1e-08 to 1e-06
Outputs:
- loss: float32 [], replicated
- input_grads: bfloat16 [4, 512, 6656], P('section', None, 'tensor')
- new_weights: bfloat16 [4, 6656, 6656], P('section', 'tensor')
- new_row_state: float32 [4, 6656], P('section', 'tensor')
- new_col_state: float32 [4, 6656], P('section')
All inputs are finite; a program needn't handle non-finite values.
Results may differ from a plain program's by a relative error of at most 0.007.
Values may be sent and summed in bfloat16 or wider, within the bound.
A program may use at most 192 MiB of HBM per device.

v0:
```python
import jax
import jax.numpy as jnp
from jax import lax
from jax.sharding import PartitionSpec as P

decay_rate = 0.9
learn_rate = 0.3
tiny_term = 1e-30


def shifted(block, axis, distance):
    devices = range(lax.axis_size(axis))
    route = [(i - distance, i) for i in devices if i - distance in devices]
    return lax.ppermute(block, axis, route)


def body(hidden_last, labels, head_weight, layer_inputs, weights, row_state, col_state):
    section_count = lax.axis_size("section")
    section_index = lax.axis_index("section")
    all_rows = labels.shape[0]
    model_width = head_weight.shape[0]
    vocab_local = head_weight.shape[1]
    local_weight = weights[0]
    rows_local = local_weight.shape[0]
    saved_all = layer_inputs[0]
    columns = lax.axis_index("tensor") * vocab_local + lax.iota(jnp.int32, vocab_local)
    share_rows = all_rows // section_count
    row_start = section_index * share_rows
    hidden_rows = lax.dynamic_slice_in_dim(hidden_last, row_start, share_rows, 0)
    head_slice = head_weight
    logits = jnp.dot(
        lax.all_gather(hidden_rows, "tensor", axis=1, tiled=True),
        head_slice,
        preferred_element_type=jnp.float32,
    )
    exponent = jnp.exp(logits)
    label_hit = (
        lax.dynamic_slice_in_dim(labels, row_start, share_rows, 0)[:, None] == columns[None, :]
    )
    denominator, picked = lax.psum(
        (
            jnp.sum(exponent, axis=1),
            jnp.sum(jnp.where(label_hit, logits, jnp.zeros_like(logits)), axis=1),
        ),
        "tensor",
    )
    losses = jnp.log(denominator) - picked
    logit_grad = (
        (exponent / denominator[:, None] - label_hit.astype(jnp.float32)) / all_rows
    ).astype(jnp.bfloat16)
    head_slice = head_weight
    shares = lax.psum_scatter(
        lax.dot_general(
            head_slice, logit_grad, (((1,), (1,)), ((), ())), preferred_element_type=jnp.float32
        ),
        "tensor",
        scatter_dimension=0,
        tiled=True,
    )
    part_grad = shares.T.astype(jnp.bfloat16)
    part_loss = jnp.sum(losses)
    head_grad = lax.all_gather(part_grad, "section", axis=0, tiled=True)
    loss = lax.psum(part_loss, "section") / all_rows
    is_last = section_index == section_count - 1

    def layer_block(dy_rows, saved_rows):
        gathered = lax.all_gather(dy_rows, "tensor", axis=1, tiled=True)
        backward = lax.dot_general(
            gathered, local_weight, (((1,), (1,)), ((), ())), preferred_element_type=jnp.float32
        )
        product = lax.dot_general(
            saved_rows, gathered, (((0,), (0,)), ((), ())), preferred_element_type=jnp.float32
        )
        backward, piece_grad = (backward, product)
        input_grad = (dy_rows.astype(jnp.float32) + backward).astype(jnp.bfloat16)
        return (input_grad, piece_grad)

    start_grad = jnp.zeros((rows_local, model_width), jnp.float32)

    def advance_whole(step_index, loop_state):
        received, gradient, outputs = loop_state
        active = step_index == section_count - 1 - section_index
        dy_rows = jnp.where(is_last, head_grad, received)
        input_grad, piece_grad = layer_block(dy_rows, saved_all)
        gradient = gradient + jnp.where(active, piece_grad, jnp.zeros_like(piece_grad))
        outputs = jnp.where(active, input_grad, outputs)
        received = shifted(input_grad, "section", -1)
        return (received, gradient, outputs)

    loop_state = (
        jnp.zeros((all_rows, rows_local), jnp.bfloat16),
        start_grad,
        jnp.zeros((all_rows, rows_local), jnp.bfloat16),
    )
    loop_state = lax.fori_loop(0, section_count, advance_whole, loop_state)
    gradient = loop_state[1]
    outputs = loop_state[2]
    weight_float = local_weight.astype(jnp.float32)
    squares = gradient * gradient + tiny_term
    row_new = decay_rate * row_state[0] + (1.0 - decay_rate) * jnp.mean(squares, axis=1)
    col_part = jnp.sum(squares, axis=0)
    entries = float(model_width * model_width)
    col_sum, row_total, weight_total = lax.psum(
        (col_part, jnp.sum(row_new), jnp.sum(weight_float * weight_float)), "tensor"
    )
    col_new = decay_rate * col_state[0] + (1.0 - decay_rate) * (col_sum / model_width)
    update = gradient / jnp.sqrt(row_new[:, None] * col_new[None, :] / row_total)
    update_total = lax.psum(jnp.sum(update * update), "tensor")
    factor = (
        learn_rate
        * jnp.sqrt(weight_total / entries)
        / jnp.maximum(1.0, jnp.sqrt(update_total / entries))
    )
    new_weight = (weight_float - factor * update).astype(jnp.bfloat16)
    return (loss, outputs[None], new_weight[None], row_new[None], col_new[None])


def solution(mesh):
    return jax.shard_map(
        body,
        mesh=mesh,
        in_specs=(
            P(None, "tensor"),
            P(),
            P(None, "tensor"),
            P("section", None, "tensor"),
            P("section", "tensor", None),
            P("section", "tensor"),
            P("section", None),
        ),
        out_specs=(
            P(),
            P("section", None, "tensor"),
            P("section", "tensor", None),
            P("section", "tensor"),
            P("section", None),
        ),
        check_vma=False,
    )
```

profile of v0, /device:TPU:0, one launch (start us, length us, event | category | flops | bytes accessed | tf_op | source)
XLA Modules:
  0.0 680.5 jit_solution(17623979021237377767)
XLA Ops:
  9.9 29.1 %all-gather.3.cloned.1.call-done = bf16[128,6656]{0,1:T(8,128)(2,1)} async-done(((bf16[128,832]{0,1:T(8,128)(2,1)}), bf16[128,6656]{0,1:T(8,128)(2,1)}) %all-gather.3.cloned.1.call-update) | async-done | bytes 1703952 | tf_op jit(solution)/shard_map/all_gather | solution.py:32
  39.0 22.1 %exponential_reduce_fusion = (f32[128]{0:T(128)S(1)}, f32[128]{0:T(128)}, f32[128,4000]{0,1:T(8,128)S(1)}) fusion(s32[4000]{0:T(1024)S(1)} %iota_add_fusion, s32[128]{0:T(128)S(1)} %dynamic_slice.7, bf16[6656,4000]{0,1:T(8,128)(2,1)} %param.11, bf16[128,6656]{0,1:T(8,128)(2,1)} %all-gather.3.cloned.1.call-done), kind=kOutput, calls=%fused_computation.21 | convolution fusion | flops 6817792000 | bytes 57017472 | tf_op jit(solution)/shard_map/dot_general | solution.py:31
  61.0 15.1 %psum.49 = f32[128]{0:T(128)S(1)} all-reduce(f32[128]{0:T(128)S(1)} %get-tuple-element.270), channel_id=1, replica_groups=mesh['section'=4,'tensor'=8] {'tensor'}, use_global_device_ids=true, to_apply=%region_1.2 | all-reduce | flops 128 | bytes 1024 | tf_op jit(solution)/shard_map/psum | solution.py:40
  76.2 20.9 %convolution_bitcast_fusion = f32[6656,128]{0,1:T(8,128)} fusion(bf16[6656,4000]{0,1:T(8,128)(2,1)} %param.11, f32[128,4000]{0,1:T(8,128)S(1)} %get-tuple-element.300, f32[128]{0:T(128)S(1)} %psum.49, s32[128]{0:T(128)S(1)} %dynamic_slice.7, s32[4000]{0:T(1024)S(1)} %iota_add_fusion), kind=kOutput, calls=%fused_computation.14 | convolution fusion | flops 6818816000 | bytes 58720896 | tf_op jit(solution)/shard_map/dot_general | solution.py:53
  104.1 10.8 %fusion = f32[]{:T(128)} fusion(bf16[1,832,6656]{2,1,0:T(8,128)(2,1)} %param.13), kind=kLoop, calls=%fused_computation.6 | loop fusion | flops 16613375 | bytes 11075588 | tf_op jit(solution)/shard_map/reduce_sum | solution.py:104
  114.9 28.1 %reduce-scatter.4.cloned.1.call-done = f32[832,128]{1,0:T(8,128)} async-done(((f32[6656,128]{1,0:T(8,128)}), f32[832,128]{1,0:T(8,128)}) %reduce-scatter.4.cloned.1.call-update) | async-done | bytes 426000
  144.1 12.6 %all_gather.16 = bf16[512,832]{1,0:T(8,128)(2,1)S(1)} all-gather(bf16[128,832]{1,0:T(8,128)(2,1)S(1)} %bitcast.35), channel_id=1, replica_groups=mesh['section'=4,'tensor'=8] {'section'}, dimensions={0}, use_global_device_ids=true | all-gather | bytes 1064960 | tf_op jit(solution)/shard_map/all_gather | solution.py:62
  157.3 420.9 %while.20 = (s32[]{:T(128)}, bf16[512,832]{0,1:T(8,128)(2,1)S(1)}, f32[832,6656]{1,0:T(8,128)}, bf16[512,832]{0,1:T(8,128)(2,1)}, pred[]{:T(512)}, /*index=5*/bf...) while((s32[]{:T(128)}, bf16[512,832]{0,1:T(8,128)(2,1)S(1)}, ...), condition=%wide.region_8.9_spmd.clone, body=%wide.region_7.8_spmd.clone.sunk | while | flops 11360567296 | bytes 102236368 | solution.py:95
  158.4 70.2 %all-gather.5.cloned.1.call-done = bf16[512,6656]{0,1:T(8,128)(2,1)} async-done(((bf16[512,832]{0,1:T(8,128)(2,1)}), bf16[512,6656]{0,1:T(8,128)(2,1)}) %all-gather.5.cloned.1.call-update) | async-done | bytes 6815760 | tf_op jit(solution)/shard_map/while/body/eval_jaxpr/all_gather | solution.py:67
  228.6 11.6 %select_select_fusion.2 = (bf16[512,832]{0,1:T(8,128)(2,1)}, bf16[512,832]{0,1:T(8,128)(2,1)S(1)}) fusion(bf16[512,832]{0,1:T(8,128)(2,1)} %get-tuple-element.374, pred[]{:T(512)S(6)} %compare.3, pred[]{:T(512)S(6)} %eq.52, bf16[832,6656]{1,0:T(8,128)(2,1)} %get-tuple-element.388, bf16[512,6656]{0,1:T(8,128)(2,1)} %all-gather.5.cloned.1.call-done, ...), kind=kOutput, calls=%fused_computation.2.clone.1 | convolution fusion | flops 5672828928 | bytes 21299202 | tf_op jit(solution)/shard_map/while/body/eval_jaxpr/dot_general | solution.py:68
  241.4 12.6 %bitcast_add_fusion.2 = f32[832,6656]{1,0:T(8,128)} fusion(f32[832,6656]{1,0:T(8,128)} %get-tuple-element.373, bf16[512,6656]{0,1:T(8,128)(2,1)} %all-gather.5.cloned.1.call-done, bf16[512,832]{1,0:T(8,128)(2,1)S(1)} %get-tuple-element.390, pred[]{:T(512)S(6)} %compare.3, pred[]{:T(512)S(6)} %eq.52), kind=kOutput, calls=%fused_computation.clone.1 | convolution fusion | flops 5687312384 | bytes 51970048 | tf_op jit(solution)/shard_map/while/body/eval_jaxpr/dot_general | solution.py:71
  264.1 69.3 %all-gather.5.cloned.1.call-done = bf16[512,6656]{0,1:T(8,128)(2,1)} async-done(((bf16[512,832]{0,1:T(8,128)(2,1)}), bf16[512,6656]{0,1:T(8,128)(2,1)}) %all-gather.5.cloned.1.call-update) | async-done | bytes 6815760 | tf_op jit(solution)/shard_map/while/body/eval_jaxpr/all_gather | solution.py:67
  333.5 11.7 %select_select_fusion.2 = (bf16[512,832]{0,1:T(8,128)(2,1)}, bf16[512,832]{0,1:T(8,128)(2,1)S(1)}) fusion(bf16[512,832]{0,1:T(8,128)(2,1)} %get-tuple-element.374, pred[]{:T(512)S(6)} %compare.3, pred[]{:T(512)S(6)} %eq.52, bf16[832,6656]{1,0:T(8,128)(2,1)} %get-tuple-element.388, bf16[512,6656]{0,1:T(8,128)(2,1)} %all-gather.5.cloned.1.call-done, ...), kind=kOutput, calls=%fused_computation.2.clone.1 | convolution fusion | flops 5672828928 | bytes 21299202 | tf_op jit(solution)/shard_map/while/body/eval_jaxpr/dot_general | solution.py:68
  346.5 16.7 %bitcast_add_fusion.2 = f32[832,6656]{1,0:T(8,128)} fusion(f32[832,6656]{1,0:T(8,128)} %get-tuple-element.373, bf16[512,6656]{0,1:T(8,128)(2,1)} %all-gather.5.cloned.1.call-done, bf16[512,832]{1,0:T(8,128)(2,1)S(1)} %get-tuple-element.390, pred[]{:T(512)S(6)} %compare.3, pred[]{:T(512)S(6)} %eq.52), kind=kOutput, calls=%fused_computation.clone.1 | convolution fusion | flops 5687312384 | bytes 51970048 | tf_op jit(solution)/shard_map/while/body/eval_jaxpr/dot_general | solution.py:71
  369.2 69.3 %all-gather.5.cloned.1.call-done = bf16[512,6656]{0,1:T(8,128)(2,1)} async-done(((bf16[512,832]{0,1:T(8,128)(2,1)}), bf16[512,6656]{0,1:T(8,128)(2,1)}) %all-gather.5.cloned.1.call-update) | async-done | bytes 6815760 | tf_op jit(solution)/shard_map/while/body/eval_jaxpr/all_gather | solution.py:67
  438.5 11.7 %select_select_fusion.2 = (bf16[512,832]{0,1:T(8,128)(2,1)}, bf16[512,832]{0,1:T(8,128)(2,1)S(1)}) fusion(bf16[512,832]{0,1:T(8,128)(2,1)} %get-tuple-element.374, pred[]{:T(512)S(6)} %compare.3, pred[]{:T(512)S(6)} %eq.52, bf16[832,6656]{1,0:T(8,128)(2,1)} %get-tuple-element.388, bf16[512,6656]{0,1:T(8,128)(2,1)} %all-gather.5.cloned.1.call-done, ...), kind=kOutput, calls=%fused_computation.2.clone.1 | convolution fusion | flops 5672828928 | bytes 21299202 | tf_op jit(solution)/shard_map/while/body/eval_jaxpr/dot_general | solution.py:68
  451.5 16.7 %bitcast_add_fusion.2 = f32[832,6656]{1,0:T(8,128)} fusion(f32[832,6656]{1,0:T(8,128)} %get-tuple-element.373, bf16[512,6656]{0,1:T(8,128)(2,1)} %all-gather.5.cloned.1.call-done, bf16[512,832]{1,0:T(8,128)(2,1)S(1)} %get-tuple-element.390, pred[]{:T(512)S(6)} %compare.3, pred[]{:T(512)S(6)} %eq.52), kind=kOutput, calls=%fused_computation.clone.1 | convolution fusion | flops 5687312384 | bytes 51970048 | tf_op jit(solution)/shard_map/while/body/eval_jaxpr/dot_general | solution.py:71
  474.2 69.3 %all-gather.5.cloned.1.call-done = bf16[512,6656]{0,1:T(8,128)(2,1)} async-done(((bf16[512,832]{0,1:T(8,128)(2,1)}), bf16[512,6656]{0,1:T(8,128)(2,1)}) %all-gather.5.cloned.1.call-update) | async-done | bytes 6815760 | tf_op jit(solution)/shard_map/while/body/eval_jaxpr/all_gather | solution.py:67
  543.6 11.7 %select_select_fusion.2 = (bf16[512,832]{0,1:T(8,128)(2,1)}, bf16[512,832]{0,1:T(8,128)(2,1)S(1)}) fusion(bf16[512,832]{0,1:T(8,128)(2,1)} %get-tuple-element.374, pred[]{:T(512)S(6)} %compare.3, pred[]{:T(512)S(6)} %eq.52, bf16[832,6656]{1,0:T(8,128)(2,1)} %get-tuple-element.388, bf16[512,6656]{0,1:T(8,128)(2,1)} %all-gather.5.cloned.1.call-done, ...), kind=kOutput, calls=%fused_computation.2.clone.1 | convolution fusion | flops 5672828928 | bytes 21299202 | tf_op jit(solution)/shard_map/while/body/eval_jaxpr/dot_general | solution.py:68
  556.6 16.7 %bitcast_add_fusion.2 = f32[832,6656]{1,0:T(8,128)} fusion(f32[832,6656]{1,0:T(8,128)} %get-tuple-element.373, bf16[512,6656]{0,1:T(8,128)(2,1)} %all-gather.5.cloned.1.call-done, bf16[512,832]{1,0:T(8,128)(2,1)S(1)} %get-tuple-element.390, pred[]{:T(512)S(6)} %compare.3, pred[]{:T(512)S(6)} %eq.52), kind=kOutput, calls=%fused_computation.clone.1 | convolution fusion | flops 5687312384 | bytes 51970048 | tf_op jit(solution)/shard_map/while/body/eval_jaxpr/dot_general | solution.py:71
  588.6 26.0 %all-reduce.1 = (f32[]{:T(128)}, f32[6656]{0:T(1024)S(1)}) all-reduce(f32[]{:T(128)} %get-tuple-element.295, f32[6656]{0:T(1024)S(1)} %get-tuple-element.268), channel_id=1, replica_groups=mesh['section'=4,'tensor'=8] {'tensor'}, use_global_device_ids=true, to_apply=%region_15.16 | all-reduce | flops 6657 | bytes 53256 | tf_op jit(solution)/shard_map/psum | solution.py:103
  614.6 11.9 %multiply_reduce_fusion = f32[]{:T(128)} fusion(f32[832,6656]{1,0:T(8,128)} %get-tuple-element.219, f32[]{:T(128)} %get-tuple-element.293, f32[6656]{0:T(1024)S(1)} %multiply_add_fusion.1, f32[832]{0:T(1024)S(1)} %get-tuple-element.296), kind=kLoop, calls=%fused_computation.8 | loop fusion | flops 27688960 | bytes 22181128 | tf_op jit(solution)/shard_map/reduce_sum | solution.py:108
  626.5 14.2 %all-reduce = (f32[128]{0:T(128)S(1)}, f32[]{:T(128)}, f32[]{:T(128)}) all-reduce(f32[128]{0:T(128)S(1)} %copy-done.10, f32[]{:T(128)} %fusion, f32[]{:T(128)} %multiply_reduce_fusion), channel_id=1, replica_groups=mesh['section'=4,'tensor'=8] {'tensor'}, use_global_device_ids=true, to_apply=%region_3.4 | all-reduce | flops 130 | bytes 1040 | tf_op jit(solution)/shard_map/psum | solution.py:40
  642.2 17.4 %fusion.4 = bf16[1,832,6656]{2,1,0:T(8,128)(2,1)} fusion(f32[]{:T(128)S(6)} %div.49, bf16[1,832,6656]{2,1,0:T(8,128)(2,1)} %bitcast.33, f32[832,6656]{1,0:T(8,128)} %get-tuple-element.219, f32[]{:T(128)} %get-tuple-element.293, f32[6656]{0:T(1024)S(1)} %multiply_add_fusion.1, f32[832]{0:T(1024)S(1)} %get-tuple-element.296), kind=kLoop, calls=%fused_computation.13 | loop fusion | flops 38764544 | bytes 44332296 | tf_op jit(solution)/shard_map/broadcast_in_dim | solution.py:115
  (65 shorter events, 67.3 us)
Async XLA Ops:
  7.2 1.2 copy-start
  7.2 31.8 %all-gather.3.cloned.1.call-start = ((), (), s32[]{:S(2)}) async-start(), calls=%async_computation.1 | async-start | bytes 1916928 | tf_op jit(solution)/shard_map/all_gather | solution.py:32
  9.1 133.9 %reduce-scatter.4.cloned.1.call-start = ((), (), s32[]{:S(2)}) async-start(), calls=%async_computation.2 | async-start | bytes 3833856
  76.2 20.9 %copy-start.8 = (f32[128]{0:T(128)}, f32[128]{0:T(128)S(1)}, u32[]{:S(2)}) copy-start(f32[128]{0:T(128)S(1)} %psum.49) | copy-start | bytes 1540
  76.2 26.0 %copy-start.2 = (bf16[1,512,832]{1,2,0:T(8,128)(2,1)S(1)}, bf16[1,512,832]{1,2,0:T(8,128)(2,1)}, u32[]{:S(2)}) copy-start(bf16[1,512,832]{1,2,0:T(8,128)(2,1)} %param.12) | copy-start | bytes 2555908
  76.2 26.6 %copy-start.6 = (f32[1,832]{1,0:T(1,128)S(1)}, f32[1,832]{1,0:T(1,128)}, u32[]{:S(2)}) copy-start(f32[1,832]{1,0:T(1,128)} %param.14) | copy-start | bytes 9988
  76.2 27.2 %copy-start.4 = (f32[1,6656]{1,0:T(1,128)S(1)}, f32[1,6656]{1,0:T(1,128)}, u32[]{:S(2)}) copy-start(f32[1,6656]{1,0:T(1,128)} %param.15) | copy-start | bytes 79876
  157.3 71.2 %all-gather.5.cloned.1.call-start = ((), (), s32[]{:S(2)}) async-start(), calls=%async_computation.3 | async-start | bytes 7667712 | tf_op jit(solution)/shard_map/while/body/eval_jaxpr/all_gather | solution.py:67
  240.1 23.0 %collective-permute-start = (bf16[512,832]{0,1:T(8,128)(2,1)S(1)}, bf16[512,832]{0,1:T(8,128)(2,1)S(1)}, u32[]{:S(2)}, u32[]{:S(2)}) collective-permute-start(bf16[512,832]{0,1:T(8,128)(2,1)S(1)} %get-tuple-element.358), channel_id=1, source_target_pairs={{8,0},{16,8},{24,16},{9,1},{17,9},{25,17},{10,2},{18,10},{26,18},{... | collective-permute-start | bytes 2555912 | tf_op jit(solution)/shard_map/while/body/eval_jaxpr/ppermute | solution.py:14
  263.1 70.4 %all-gather.5.cloned.1.call-start = ((), (), s32[]{:S(2)}) async-start(), calls=%async_computation.3 | async-start | bytes 7667712 | tf_op jit(solution)/shard_map/while/body/eval_jaxpr/all_gather | solution.py:67
  345.2 23.0 %collective-permute-start = (bf16[512,832]{0,1:T(8,128)(2,1)S(1)}, bf16[512,832]{0,1:T(8,128)(2,1)S(1)}, u32[]{:S(2)}, u32[]{:S(2)}) collective-permute-start(bf16[512,832]{0,1:T(8,128)(2,1)S(1)} %get-tuple-element.358), channel_id=1, source_target_pairs={{8,0},{16,8},{24,16},{9,1},{17,9},{25,17},{10,2},{18,10},{26,18},{... | collective-permute-start | bytes 2555912 | tf_op jit(solution)/shard_map/while/body/eval_jaxpr/ppermute | solution.py:14
  368.2 70.4 %all-gather.5.cloned.1.call-start = ((), (), s32[]{:S(2)}) async-start(), calls=%async_computation.3 | async-start | bytes 7667712 | tf_op jit(solution)/shard_map/while/body/eval_jaxpr/all_gather | solution.py:67
  450.2 23.0 %collective-permute-start = (bf16[512,832]{0,1:T(8,128)(2,1)S(1)}, bf16[512,832]{0,1:T(8,128)(2,1)S(1)}, u32[]{:S(2)}, u32[]{:S(2)}) collective-permute-start(bf16[512,832]{0,1:T(8,128)(2,1)S(1)} %get-tuple-element.358), channel_id=1, source_target_pairs={{8,0},{16,8},{24,16},{9,1},{17,9},{25,17},{10,2},{18,10},{26,18},{... | collective-permute-start | bytes 2555912 | tf_op jit(solution)/shard_map/while/body/eval_jaxpr/ppermute | solution.py:14
  473.2 70.4 %all-gather.5.cloned.1.call-start = ((), (), s32[]{:S(2)}) async-start(), calls=%async_computation.3 | async-start | bytes 7667712 | tf_op jit(solution)/shard_map/while/body/eval_jaxpr/all_gather | solution.py:67
  555.3 23.0 %collective-permute-start = (bf16[512,832]{0,1:T(8,128)(2,1)S(1)}, bf16[512,832]{0,1:T(8,128)(2,1)S(1)}, u32[]{:S(2)}, u32[]{:S(2)}) collective-permute-start(bf16[512,832]{0,1:T(8,128)(2,1)S(1)} %get-tuple-element.358), channel_id=1, source_target_pairs={{8,0},{16,8},{24,16},{9,1},{17,9},{25,17},{10,2},{18,10},{26,18},{... | collective-permute-start | bytes 2555912 | tf_op jit(solution)/shard_map/while/body/eval_jaxpr/ppermute | solution.py:14
  578.2 9.7 %copy-start.5 = (f32[832]{0:T(1024)S(1)}, f32[832]{0:T(1024)}, u32[]{:S(2)}) copy-start(f32[832]{0:T(1024)} %multiply_reduce_fusion.2) | copy-start | bytes 9988
  578.2 36.4 %copy-start.3 = (f32[6656]{0:T(1024)S(1)}, f32[6656]{0:T(1024)}, u32[]{:S(2)}) copy-start(f32[6656]{0:T(1024)} %multiply_reduce_fusion.1) | copy-start | bytes 79876
  578.3 48.3 %copy-start.10 = (f32[128]{0:T(128)S(1)}, f32[128]{0:T(128)}, u32[]{:S(2)}) copy-start(f32[128]{0:T(128)} %get-tuple-element.271) | copy-start | bytes 1540
  642.1 30.4 %copy-start.1 = (bf16[512,832]{0,1:T(8,128)(2,1)S(1)}, bf16[512,832]{0,1:T(8,128)(2,1)}, u32[]{:S(2)}) copy-start(bf16[512,832]{0,1:T(8,128)(2,1)} %param.9) | copy-start | bytes 2555908
  642.2 17.4 %copy-start.9 = (f32[128]{0:T(128)S(1)}, f32[128]{0:T(128)}, u32[]{:S(2)}) copy-start(f32[128]{0:T(128)} %copy-done.8) | copy-start | bytes 1540
  642.2 29.1 %copy-start.7 = (f32[1,832]{1,0:T(1,128)S(1)}, f32[1,832]{1,0:T(1,128)}, u32[]{:S(2)}) copy-start(f32[1,832]{1,0:T(1,128)} %param.14) | copy-start | bytes 9988
Sparse Core Ops, SparseCore 0:
  10.2 28.7 all-gather.2
  102.3 40.6 reduce-scatter.3
  160.3 68.1 all-gather.4
  265.8 67.6 all-gather.4
  370.9 67.6 all-gather.4
  475.9 67.6 all-gather.4
where the time goes:
time: 681 us
  waiting for transfers between devices  360 us (53%)
  matrix products  152 us (22%)
  blocking collectives  78.4 us (12%)
  other arithmetic  56.9 us (8%)
  between operations  17.4 us (3%)
  local copies, waits for them, and re-layouts  10.6 us (2%)
    all_gather x4, waiting for transfers between devices, layer_block(): gathered = lax.all_gather(dy_rows, 'tensor', axis=1, tiled=True)  278 us
    dot_general x4, matrix products, layer_block(): lax.dot_general(saved_rows, gathered, (((0,), (0,)), ((), ())), preferred...  62.6 us
    dot_general x4, matrix products, layer_block(): lax.dot_general(gathered, local_weight, (((1,), (1,)), ((), ())), preferr...  46.7 us
    psum x2, blocking collectives, body(): lax.psum((jnp.sum(exponent, axis=1), jnp.sum(jnp.where(label_hit, logits,...  29.4 us
    all_gather x1, waiting for transfers between devices, body(): lax.all_gather(hidden_rows, 'tensor', axis=1, tiled=True)  29.1 us
    unnamed x3, waiting for transfers between devices  28.1 us
    psum x1, blocking collectives, body(): lax.psum((col_part, jnp.sum(row_new), jnp.sum(weight_float * weight_float...  26 us
    ppermute x4, waiting for transfers between devices, shifted(): return lax.ppermute(block, axis, route)  24.1 us
  transfers between devices with their start and end apart: 10, of which 10 were waited for; matrix products, arithmetic and copies ran while one was open for 11% of the time, Pallas kernels for 0%

commit v1 on v0

v1 whole, which is shorter than its diff:
```python
import functools

import jax
import jax.numpy as jnp
from jax import lax
from jax.experimental import pallas as pl
from jax.experimental.pallas import tpu as pltpu
from jax.sharding import PartitionSpec as P

decay_rate = 0.9
learn_rate = 0.3
tiny_term = 1e-30


MESH = pl.DeviceIdType.MESH


def chain_kernel(
    sections, tensors, part_ref, loss_ref, w_ref, out_ref, g_ref, total_ref,
    loss_buf, send_x, recv_x, send_ring, recv_ring, send_mate, recv_mate, send_loss, recv_loss, head_sem,
):
    section = lax.axis_index("section")
    me = lax.axis_index("tensor")
    chips = tensors // 2
    chip, core = me // 2, me % 2
    right = lax.rem(chip + 1, chips) * 2 + core
    left = lax.rem(chip + chips - 1, chips) * 2 + core
    mate = chip * 2 + 1 - core
    features, lanes = part_ref.shape
    half = features // 2 // 16 * 16
    last = sections - 1
    reach = chips // 2

    def block(share, origin, low, size):
        rows = pl.ds(pl.multiple_of(origin * features + low, 16), size)
        return g_ref.at[rows, pl.ds(pl.multiple_of(share * lanes, lanes), lanes)]

    def span(way, distance):
        if 2 * distance < chips:
            return 0, features
        return (0, half) if way == 0 else (half, features - half)

    def remote(src, dst, send, recv, device):
        return pltpu.make_async_remote_copy(
            src_ref=src, dst_ref=dst, send_sem=send, recv_sem=recv, device_id=device, device_id_type=MESH
        )

    def origin_of(way, distance):
        there = chip - distance if way == 0 else chip + distance
        return lax.rem(there + chips, chips) * 2 + core

    def ring_copy(share, way, distance, origin):
        low, size = span(way, distance)
        where = block(share, origin, low, size)
        slot = (share, way * reach + distance - 1)
        return remote(
            where, where, send_ring.at[slot], recv_ring.at[slot], {"tensor": right if way == 0 else left}
        )

    def mate_copy(share, way, distance, origin):
        low, size = (0, features) if distance == 0 else span(way, distance)
        where = block(share, origin, low, size)
        slot = (share, 0 if distance == 0 else 1 + way * reach + distance - 1)
        return remote(where, where, send_mate.at[slot], recv_mate.at[slot], {"tensor": mate})

    def down_copy(share):
        columns = pl.ds(pl.multiple_of(share * lanes, lanes), lanes)
        below = jnp.maximum(section - 1, 0)
        return remote(
            out_ref.at[:, columns], block(share, me, 0, features),
            send_x.at[share], recv_x.at[share], {"section": below},
        )

    def head_copy():
        return remote(
            part_ref, block(section, me, 0, features), head_sem.at[0], recv_x.at[section], {"section": last}
        )

    def own_copy():
        return pltpu.make_async_copy(part_ref, block(last, me, 0, features), head_sem.at[1])

    def loss_copy(step):
        other = lax.rem(section + step, sections)
        return remote(
            loss_ref, loss_buf.at[step - 1], send_loss.at[step - 1], recv_loss.at[step - 1], {"section": other}
        )

    barrier = pltpu.get_barrier_semaphore()
    greeted = [{"tensor": mate}]
    if reach:
        greeted += [{"tensor": right}, {"tensor": left}]
    greeted += [{"section": lax.rem(section + step, sections)} for step in range(1, sections)]
    for device in greeted:
        pl.semaphore_signal(barrier, inc=1, device_id=device, device_id_type=MESH)
    pl.semaphore_wait(barrier, len(greeted))

    @pl.when(section == last)
    def _():
        own_copy().start()

    @pl.when(section != last)
    def _():
        head_copy().start()

    for step in range(1, sections):
        loss_copy(step).start()

    tile = features // 2 if features > 416 else features

    def advance(share, carry):
        @pl.when((section == last) & (share == last))
        def _():
            own_copy().wait()

        @pl.when((section != last) | (share != last))
        def _():
            down_copy(share).wait_recv()

        if reach:
            ring_copy(share, 0, 1, me).start()
            ring_copy(share, 1, 1, me).start()
        mate_copy(share, 0, 0, me).start()
        for distance in range(1, reach + 1):
            for way in (0, 1):
                origin = origin_of(way, distance)
                ring_copy(share, way, distance, origin).wait_recv()
                if distance < reach:
                    ring_copy(share, way, distance + 1, origin).start()
                mate_copy(share, way, distance, origin).start()
        other = 1 - 2 * core
        mate_copy(share, 0, 0, me + other).wait_recv()
        for distance in range(1, reach + 1):
            for way in (0, 1):
                mate_copy(share, way, distance, origin_of(way, distance) + other).wait_recv()
        columns = pl.ds(pl.multiple_of(share * lanes, lanes), lanes)

        def rows_step(index, inner):
            rows = pl.ds(pl.multiple_of(index * tile, 16), tile)
            mine = g_ref[pl.ds(pl.multiple_of(me * features + index * tile, 16), tile), columns]
            product = jnp.dot(w_ref[rows, :], g_ref[:, columns], preferred_element_type=jnp.float32)
            out_ref[rows, columns] = (mine.astype(jnp.float32) + product).astype(out_ref.dtype)
            return inner

        lax.fori_loop(0, features // tile, rows_step, 0)

        @pl.when(section > 0)
        def _():
            down_copy(share).start()

        return carry

    lax.fori_loop(0, sections, advance, 0)

    total = loss_ref[...]
    for step in range(1, sections):
        loss_copy(step).wait_recv()
        total = total + loss_buf[step - 1]
    total_ref[...] = total

    def finish(share, carry):
        @pl.when(section > 0)
        def _():
            down_copy(share).wait_send()

        if reach:
            ring_copy(share, 0, 1, me).wait_send()
            ring_copy(share, 1, 1, me).wait_send()
        mate_copy(share, 0, 0, me).wait_send()
        for distance in range(1, reach + 1):
            for way in (0, 1):
                origin = origin_of(way, distance)
                if distance < reach:
                    ring_copy(share, way, distance + 1, origin).wait_send()
                mate_copy(share, way, distance, origin).wait_send()
        return carry

    lax.fori_loop(0, sections, finish, 0)
    for step in range(1, sections):
        loss_copy(step).wait_send()

    @pl.when(section != last)
    def _():
        head_copy().wait_send()


def chain(part_grad, part_loss, local_weight):
    sections, tensors = lax.axis_size("section"), lax.axis_size("tensor")
    features, lanes = part_grad.shape
    width = features * tensors
    rows = lanes * sections
    ring = max(2 * (tensors // 4), 1)
    dma = pltpu.SemaphoreType.DMA
    vmem = pl.BlockSpec(memory_space=pltpu.VMEM)
    return pl.pallas_call(
        functools.partial(chain_kernel, sections, tensors),
        out_shape=(
            jax.ShapeDtypeStruct((features, rows), jnp.bfloat16),
            jax.ShapeDtypeStruct((width, rows), jnp.bfloat16),
            jax.ShapeDtypeStruct((8, 128), jnp.float32),
        ),
        in_specs=[vmem] * 3,
        out_specs=(vmem, vmem, vmem),
        scratch_shapes=[
            pltpu.VMEM((max(sections - 1, 1), 8, 128), jnp.float32),
            dma((sections,)),
            dma((sections,)),
            dma((sections, ring)),
            dma((sections, ring)),
            dma((sections, ring + 1)),
            dma((sections, ring + 1)),
            dma((max(sections - 1, 1),)),
            dma((max(sections - 1, 1),)),
            dma((2,)),
        ],
        compiler_params=pltpu.CompilerParams(
            collective_id=0, has_side_effects=True, vmem_limit_bytes=48 * 1024 * 1024
        ),
    )(part_grad, jnp.full((8, 128), part_loss, jnp.float32), local_weight)


def body(hidden_last, labels, head_weight, layer_inputs, weights, row_state, col_state):
    section_count = lax.axis_size("section")
    section_index = lax.axis_index("section")
    all_rows = labels.shape[0]
    model_width = head_weight.shape[0]
    vocab_local = head_weight.shape[1]
    local_weight = weights[0]
    rows_local = local_weight.shape[0]
    saved_all = layer_inputs[0]
    columns = lax.axis_index("tensor") * vocab_local + lax.iota(jnp.int32, vocab_local)
    share_rows = all_rows // section_count
    row_start = section_index * share_rows
    hidden_rows = lax.dynamic_slice_in_dim(hidden_last, row_start, share_rows, 0)
    head_slice = head_weight
    logits = jnp.dot(
        lax.all_gather(hidden_rows, "tensor", axis=1, tiled=True),
        head_slice,
        preferred_element_type=jnp.float32,
    )
    exponent = jnp.exp(logits)
    label_hit = (
        lax.dynamic_slice_in_dim(labels, row_start, share_rows, 0)[:, None] == columns[None, :]
    )
    denominator, picked = lax.psum(
        (
            jnp.sum(exponent, axis=1),
            jnp.sum(jnp.where(label_hit, logits, jnp.zeros_like(logits)), axis=1),
        ),
        "tensor",
    )
    losses = jnp.log(denominator) - picked
    logit_grad = (
        (exponent / denominator[:, None] - label_hit.astype(jnp.float32)) / all_rows
    ).astype(jnp.bfloat16)
    head_slice = head_weight
    shares = lax.psum_scatter(
        lax.dot_general(
            head_slice, logit_grad, (((1,), (1,)), ((), ())), preferred_element_type=jnp.float32
        ),
        "tensor",
        scatter_dimension=0,
        tiled=True,
    )
    part_grad = shares.astype(jnp.bfloat16)
    part_loss = jnp.sum(losses)
    outputs, gathered, total = chain(part_grad, part_loss, local_weight)
    loss = total[0, 0] / all_rows
    gradient = lax.dot_general(
        saved_all, gathered, (((0,), (1,)), ((), ())), preferred_element_type=jnp.float32
    )
    weight_float = local_weight.astype(jnp.float32)
    entries = float(model_width * model_width)
    square = gradient * gradient
    squares = square + tiny_term
    row_new = decay_rate * row_state[0] + (1.0 - decay_rate) * jnp.mean(squares, axis=1)
    col_part = jnp.sum(squares, axis=0)
    scaled_part = jnp.sum(square / row_new[:, None], axis=0)
    col_sum, scaled_sum, row_total, weight_total = lax.psum(
        (col_part, scaled_part, jnp.sum(row_new), jnp.sum(weight_float * weight_float)), "tensor"
    )
    col_new = decay_rate * col_state[0] + (1.0 - decay_rate) * (col_sum / model_width)
    update_total = row_total * jnp.sum(scaled_sum / col_new)
    factor = (
        learn_rate
        * jnp.sqrt(weight_total / entries)
        / jnp.maximum(1.0, jnp.sqrt(update_total / entries))
    )
    update = gradient * (lax.rsqrt(row_new)[:, None] * (lax.rsqrt(col_new) * jnp.sqrt(row_total))[None, :])
    new_weight = (weight_float - factor * update).astype(jnp.bfloat16)
    return (loss, outputs.T[None], new_weight[None], row_new[None], col_new[None])


def solution(mesh):
    return jax.shard_map(
        body,
        mesh=mesh,
        in_specs=(
            P(None, "tensor"),
            P(),
            P(None, "tensor"),
            P("section", None, "tensor"),
            P("section", "tensor", None),
            P("section", "tensor"),
            P("section", None),
        ),
        out_specs=(
            P(),
            P("section", None, "tensor"),
            P("section", "tensor", None),
            P("section", "tensor"),
            P("section", None),
        ),
        check_vma=False,
    )
```

time: 681 us -> 417 us (0.61)
  waiting for transfers between devices: 360 us -> 69.3 us
  Pallas kernels: 0 us -> 182 us
  matrix products: 152 us -> 64.9 us
  blocking collectives: 78.4 us -> 43.7 us
  other arithmetic: 56.9 us -> 33.6 us
    all_gather x4 -> x0, waiting for transfers between devices: 278 us -> none  [layer_block(): gathered = lax.all_gather(dy_rows, 'tensor', axis=1, tiled=True)]
    pallas_call x0 -> x1, Pallas kernels: none -> 182 us  [chain(): pl.pallas_call(functools.partial(chain_kernel, sections, tensors), out_sh...]
    dot_general x8 -> x1, matrix products: 109 us -> 12.5 us  [body(): lax.dot_general(saved_all, gathered, (((0,), (1,)), ((), ())), preferred_...]
    reduce_scatter x0 -> x1, waiting for transfers between devices: none -> 40.1 us  [body(): lax.psum_scatter(lax.dot_general(head_slice, logit_grad, (((1,), (1,)), (...]
    unnamed x3 -> x2, waiting for transfers between devices: 28.1 us -> 0.03 us
    ppermute x4 -> x0, waiting for transfers between devices: 24.1 us -> none  [shifted(): return lax.ppermute(block, axis, route)]
    reduce_sum x3 -> x2, other arithmetic: 32.4 us -> 14.8 us  [the longest x1 14.2 us: body(): scaled_part = jnp.sum(square / row_new[:, None], axis=0)]
    psum x2 -> x1, blocking collectives: 29.4 us -> 15.2 us  [body(): lax.psum((jnp.sum(exponent, axis=1), jnp.sum(jnp.where(label_hit, logits,...]
  transfers between devices with their start and end apart: 10 -> 2, of which waited for: 10 -> 2; matrix products, arithmetic and copies ran while one was open for 11% -> 0% of each run, Pallas kernels for 0% -> 0%
where the time goes in v1:
time: 417 us
  Pallas kernels  182 us (44%)
  waiting for transfers between devices  69.3 us (17%)
  matrix products  64.9 us (16%)
  blocking collectives  43.7 us (10%)
  other arithmetic  33.6 us (8%)
  between operations  18.7 us (4%)
  local copies, waits for them, and re-layouts  5.18 us (1%)
    pallas_call x1, Pallas kernels, chain(): pl.pallas_call(functools.partial(chain_kernel, sections, tensors), out_sh...  182 us
    reduce_scatter x1, waiting for transfers between devices, body(): lax.psum_scatter(lax.dot_general(head_slice, logit_grad, (((1,), (1,)), (...  40.1 us
    dot_general x1, matrix products, body(): lax.dot_general(head_slice, logit_grad, (((1,), (1,)), ((), ())), preferr...  29.9 us
    all_gather x1, waiting for transfers between devices, body(): lax.all_gather(hidden_rows, 'tensor', axis=1, tiled=True)  29.2 us
    psum x1, blocking collectives, body(): lax.psum((col_part, scaled_part, jnp.sum(row_new), jnp.sum(weight_float *...  28.5 us
    dot_general x1, matrix products, body(): jnp.dot(lax.all_gather(hidden_rows, 'tensor', axis=1, tiled=True), head_s...  22.5 us
    broadcast_in_dim x1, other arithmetic, body(): new_weight[None]  15.9 us
    psum x1, blocking collectives, body(): lax.psum((jnp.sum(exponent, axis=1), jnp.sum(jnp.where(label_hit, logits,...  15.2 us
  transfers between devices with their start and end apart: 2, of which 2 were waited for; matrix products, arithmetic and copies ran while one was open for 0% of the time, Pallas kernels for 0%

profile of v1, /device:TPU:0, one launch (start us, length us, event | category | flops | bytes accessed | tf_op | source)
XLA Modules:
  0.0 416.9 jit_solution(8804304674779570999)
XLA Ops:
  7.2 0.0 all-gather.2.cloned.1.call-start
  7.2 1.7 constant_dynamic-slice_fusion
  9.0 0.0 reduce-scatter.2.cloned.1.call-start
  9.0 0.8 dynamic_slice.7
  9.8 29.2 %all-gather.2.cloned.1.call-done = bf16[128,6656]{0,1:T(8,128)(2,1)} async-done(((bf16[128,832]{0,1:T(8,128)(2,1)}), bf16[128,6656]{0,1:T(8,128)(2,1)}) %all-gather.2.cloned.1.call-update) | async-done | bytes 1703952 | tf_op jit(solution)/shard_map/all_gather | solution.py:236
  39.0 22.5 %fusion.10 = (f32[128]{0:T(128)S(1)}, f32[128]{0:T(128)S(1)}, f32[128,4000]{0,1:T(8,128)}) fusion(s32[128]{0:T(128)S(1)} %dynamic_slice.7, s32[4000]{0:T(1024)S(1)} %iota_add_fusion, bf16[6656,4000]{0,1:T(8,128)(2,1)} %param.9, bf16[128,6656]{0,1:T(8,128)(2,1)} %all-gather.2.cloned.1.call-done), kind=kOutput, calls=%fused_computation.18 | convolution fusion | flops 6817792000 | bytes 57017472 | tf_op jit(solution)/shard_map/dot_general | solution.py:235
  61.5 15.2 %all-reduce.1 = (f32[128]{0:T(128)S(1)}, f32[128]{0:T(128)S(1)}) all-reduce(f32[128]{0:T(128)S(1)} %get-tuple-element.14, f32[128]{0:T(128)S(1)} %get-tuple-element.13), channel_id=1, replica_groups=mesh['section'=4,'tensor'=8] {'tensor'}, use_global_device_ids=true, to_apply=%region_1.2 | all-reduce | flops 256 | bytes 2048 | tf_op jit(solution)/shard_map/psum | solution.py:244
  76.7 29.9 %convolution_bitcast_fusion = f32[6656,128]{1,0:T(8,128)} fusion(bf16[6656,4000]{0,1:T(8,128)(2,1)} %param.9, f32[128,4000]{0,1:T(8,128)} %get-tuple-element.26, s32[128]{0:T(128)S(1)} %dynamic_slice.7, f32[128]{0:T(128)S(1)} %get-tuple-element.19, s32[4000]{0:T(1024)S(1)} %iota_add_fusion), kind=kOutput, calls=%fused_computation.12 | convolution fusion | flops 6818816000 | bytes 58720896 | tf_op jit(solution)/shard_map/dot_general | solution.py:257
  106.6 0.1 multiply_reduce_fusion
  106.7 0.6 subtract_reduce_fusion
  107.3 40.1 %reduce-scatter.2.cloned.1.call-done = f32[832,128]{1,0:T(8,128)} async-done(((f32[6656,128]{1,0:T(8,128)}), f32[832,128]{1,0:T(8,128)}) %reduce-scatter.2.cloned.1.call-update) | async-done | bytes 426000 | tf_op jit(solution)/shard_map/reduce_scatter | solution.py:256
  147.4 1.0 convert_element_type.17.part_ref
  148.4 0.6 broadcast_in_dim.11.loss_ref
  149.1 181.5 %shard_map.110 = (bf16[832,512]{1,0:T(8,128)(2,1)S(1)}, bf16[6656,512]{1,0:T(8,128)(2,1)}, f32[8,128]{1,0:T(8,128)S(1)}) custom-call(bf16[832,128]{1,0:T(8,128)(2,1)S(1)} %convert_element_type.17.part_ref, f32[8,128]{1,0:T(8,128)S(1)} %broadcast_in_dim.11.loss_ref, bf16[832,6656]{1,0:T(8,128)(2,1)} %bitcast.38), custom_call_target="tpu_custom_call" | custom-call | tf_op jit(solution)/shard_map/pallas_call | solution.py:194
  330.6 0.5 slice.3
  331.1 12.5 %fusion.5 = (f32[832]{0:T(1024)S(1)}, f32[6656,832]{0,1:T(8,128)}) fusion(bf16[6656,512]{1,0:T(8,128)(2,1)} %get-tuple-element.10, bf16[1,512,832]{1,2,0:T(8,128)(2,1)S(1)} %copy-done), kind=kOutput, calls=%fused_computation.10 | convolution fusion | flops 5687311360 | bytes 29822208 | tf_op jit(solution)/shard_map/dot_general | solution.py:268
  343.6 0.6 reshape_add_fusion
  344.2 0.6 reduce_sum.86
  344.8 14.2 %divide_reduce_fusion = (f32[6656]{0:T(1024)S(1)}, f32[6656]{0:T(1024)S(1)}, f32[]{:T(128)}) fusion(f32[6656,832]{0,1:T(8,128)} %get-tuple-element.28, f32[832]{0:T(1024)S(1)} %get-tuple-element.24, bf16[1,832,6656]{2,1,0:T(8,128)(2,1)} %param.11), kind=kLoop, calls=%fused_computation.7 | loop fusion | flops 44289024 | bytes 33283332 | tf_op jit(solution)/shard_map/reduce_sum | solution.py:277
  358.9 28.5 %all-reduce = (f32[6656]{0:T(1024)S(1)}, f32[]{:T(128)}, f32[]{:T(128)}, f32[6656]{0:T(1024)S(1)}) all-reduce(f32[6656]{0:T(1024)S(1)} %get-tuple-element.12, f32[]{:T(128)} %reduce_sum.86, f32[]{:T(128)} %get-tuple-element.29, f32[6656]{0:T(1024)S(1)} %get-tuple-element.11), channel_id=1, replica_groups=mesh['section'=4,'tensor'=8] {'tensor'}, use_global_device_ids=true, to_apply=%region_14.15 | all-reduce | flops 13314 | bytes 106512 | tf_op jit(solution)/shard_map/psum | solution.py:278
  388.8 0.6 divide_reduce_fusion.1
  390.8 0.6 broadcast_in_dim.26
  392.1 15.9 %fusion.6 = bf16[1,832,6656]{2,1,0:T(8,128)(2,1)} fusion(f32[6656,832]{0,1:T(8,128)} %get-tuple-element.28, f32[6656]{0:T(1024)S(1)} %rsqrt_multiply_fusion, f32[832]{0:T(1024)S(1)} %get-tuple-element.23, f32[]{:T(128)S(6)} %div.54, bf16[1,832,6656]{2,1,0:T(8,128)(2,1)} %param.11), kind=kLoop, calls=%fused_computation.11 | loop fusion | flops 33226752 | bytes 44332292 | tf_op jit(solution)/shard_map/broadcast_in_dim | solution.py:290
  408.1 0.9 copy.15
  (14 shorter events, 0.1 us)
Async XLA Ops:
  7.2 323.9 %copy-start = (bf16[1,512,832]{1,2,0:T(8,128)(2,1)S(1)}, bf16[1,512,832]{1,2,0:T(8,128)(2,1)}, u32[]{:S(2)}) copy-start(bf16[1,512,832]{1,2,0:T(8,128)(2,1)} %param.10) | copy-start | bytes 2555908
  7.2 31.8 %all-gather.2.cloned.1.call-start = ((), (), s32[]{:S(2)}) async-start(), calls=%async_computation.1 | async-start | bytes 1916928 | tf_op jit(solution)/shard_map/all_gather | solution.py:236
  9.0 138.4 %reduce-scatter.2.cloned.1.call-start = ((), (), s32[]{:S(2)}) async-start(), calls=%async_computation.2 | async-start | bytes 3833856 | tf_op jit(solution)/shard_map/reduce_scatter | solution.py:256
  76.7 29.9 %copy-start.3 = (f32[1,832]{1,0:T(1,128)S(1)}, f32[1,832]{1,0:T(1,128)}, u32[]{:S(2)}) copy-start(f32[1,832]{1,0:T(1,128)} %param.12) | copy-start | bytes 9988
  76.7 29.9 %copy-start.2 = (f32[1,6656]{1,0:T(1,128)S(1)}, f32[1,6656]{1,0:T(1,128)}, u32[]{:S(2)}) copy-start(f32[1,6656]{1,0:T(1,128)} %param.13) | copy-start | bytes 79876
  392.1 16.8 %copy-start.1 = (bf16[1,512,832]{1,2,0:T(8,128)(2,1)S(1)}, bf16[1,512,832]{1,2,0:T(8,128)(2,1)}, u32[]{:S(2)}) copy-start(bf16[1,512,832]{1,2,0:T(8,128)(2,1)} %param.10) | copy-start | bytes 2555908
Sparse Core Ops, SparseCore 0:
  10.2 28.7 all-gather.1
  106.7 40.6 reduce-scatter.1

commit v2 on v1

--- a/solution.py
+++ b/solution.py
@@ -16,8 +16,8 @@
 
 
 def chain_kernel(
-    sections, tensors, part_ref, loss_ref, w_ref, out_ref, g_ref, total_ref,
-    loss_buf, send_x, recv_x, send_ring, recv_ring, send_mate, recv_mate, send_loss, recv_loss, head_sem,
+    sections, tensors, part_ref, loss_ref, w_ref, out_ref, g_ref, total_ref, square_ref,
+    acc_ref, loss_buf, send_x, recv_x, send_ring, recv_ring, send_mate, recv_mate, send_loss, recv_loss, head_sem,
 ):
     section = lax.axis_index("section")
     me = lax.axis_index("tensor")
@@ -106,6 +106,24 @@
         loss_copy(step).start()
 
     tile = features // 2 if features > 416 else features
+    pair = 2 * features
+    split = pair % 128 == 0
+
+    def add_squares():
+        def rows_step(index, inner):
+            entries = w_ref[pl.ds(pl.multiple_of(index * 16, 16), 16), :].astype(jnp.float32)
+            return inner + jnp.sum(jnp.reshape(entries * entries, (2, 8, entries.shape[1])), axis=0)
+
+        width = w_ref.shape[1]
+        sums = lax.fori_loop(0, features // 16, rows_step, jnp.zeros((8, width), jnp.float32))
+        folded = sums[:, :128]
+        for start in range(128, width, 128):
+            folded = folded + sums[:, start : start + 128]
+        square_ref[...] = folded
+
+    @pl.when(section != last)
+    def _():
+        add_squares()
 
     def advance(share, carry):
         @pl.when((section == last) & (share == last))
@@ -120,6 +138,26 @@
             ring_copy(share, 0, 1, me).start()
             ring_copy(share, 1, 1, me).start()
         mate_copy(share, 0, 0, me).start()
+        columns = pl.ds(pl.multiple_of(share * lanes, lanes), lanes)
+        other = 1 - 2 * core
+
+        def product_of(owner_chip, first):
+            if owner_chip is None:
+                depth = slice(None)
+            else:
+                depth = pl.ds(pl.multiple_of(owner_chip * pair, 128), pair)
+
+            def rows_step(index, inner):
+                rows = pl.ds(pl.multiple_of(index * tile, 16), tile)
+                product = jnp.dot(w_ref[rows, depth], g_ref[depth, columns], preferred_element_type=jnp.float32)
+                acc_ref[rows, :] = product if first else acc_ref[rows, :] + product
+                return inner
+
+            lax.fori_loop(0, features // tile, rows_step, 0)
+
+        mate_copy(share, 0, 0, me + other).wait_recv()
+        if split:
+            product_of(chip, True)
         for distance in range(1, reach + 1):
             for way in (0, 1):
                 origin = origin_of(way, distance)
@@ -127,21 +165,14 @@
                 if distance < reach:
                     ring_copy(share, way, distance + 1, origin).start()
                 mate_copy(share, way, distance, origin).start()
-        other = 1 - 2 * core
-        mate_copy(share, 0, 0, me + other).wait_recv()
-        for distance in range(1, reach + 1):
             for way in (0, 1):
                 mate_copy(share, way, distance, origin_of(way, distance) + other).wait_recv()
-        columns = pl.ds(pl.multiple_of(share * lanes, lanes), lanes)
-
-        def rows_step(index, inner):
-            rows = pl.ds(pl.multiple_of(index * tile, 16), tile)
-            mine = g_ref[pl.ds(pl.multiple_of(me * features + index * tile, 16), tile), columns]
-            product = jnp.dot(w_ref[rows, :], g_ref[:, columns], preferred_element_type=jnp.float32)
-            out_ref[rows, columns] = (mine.astype(jnp.float32) + product).astype(out_ref.dtype)
-            return inner
-
-        lax.fori_loop(0, features // tile, rows_step, 0)
+                if split and (way == 1 or 2 * distance < chips):
+                    product_of(origin_of(way, distance) // 2, False)
+        if not split:
+            product_of(None, True)
+        mine = g_ref[pl.ds(pl.multiple_of(me * features, 16), features), columns]
+        out_ref[:, columns] = (mine.astype(jnp.float32) + acc_ref[...]).astype(out_ref.dtype)
 
         @pl.when(section > 0)
         def _():
@@ -150,6 +181,10 @@
         return carry
 
     lax.fori_loop(0, sections, advance, 0)
+
+    @pl.when(section == last)
+    def _():
+        add_squares()
 
     total = loss_ref[...]
     for step in range(1, sections):
@@ -181,6 +216,212 @@
     @pl.when(section != last)
     def _():
         head_copy().wait_send()
+
+
+def gather_kernel(tensors, x_ref, g_ref, send_ring, recv_ring, send_mate, recv_mate, own_sem):
+    me = lax.axis_index("tensor")
+    chips = tensors // 2
+    chip, core = me // 2, me % 2
+    right = lax.rem(chip + 1, chips) * 2 + core
+    left = lax.rem(chip + chips - 1, chips) * 2 + core
+    mate = chip * 2 + 1 - core
+    features = x_ref.shape[0]
+    half = features // 2 // 16 * 16
+    reach = chips // 2
+
+    barrier = pltpu.get_barrier_semaphore()
+    greeted = [mate] + ([right, left] if reach else [])
+    for device in greeted:
+        pl.semaphore_signal(barrier, inc=1, device_id={"tensor": device}, device_id_type=MESH)
+    pl.semaphore_wait(barrier, len(greeted))
+
+    def copy(way, distance, origin, to_mate):
+        low, size = 0, features
+        if distance and 2 * distance == chips:
+            low, size = (0, half) if way == 0 else (half, features - half)
+        where = g_ref.at[pl.ds(pl.multiple_of(origin * features + low, 16), size), :]
+        own = (distance == 0) if to_mate else (distance == 1)
+        slot = 0 if distance == 0 else way * reach + distance - 1 + int(to_mate)
+        send, recv = (send_mate, recv_mate) if to_mate else (send_ring, recv_ring)
+        target = mate if to_mate else (right if way == 0 else left)
+        return pltpu.make_async_remote_copy(
+            src_ref=x_ref.at[pl.ds(low, size), :] if own else where, dst_ref=where,
+            send_sem=send.at[slot], recv_sem=recv.at[slot],
+            device_id={"tensor": target}, device_id_type=MESH,
+        )
+
+    def origin_of(way, distance):
+        there = chip - distance if way == 0 else chip + distance
+        return lax.rem(there + chips, chips) * 2 + core
+
+    sent = []
+
+    def start(*args):
+        copy(*args).start()
+        sent.append(args)
+
+    own_block = g_ref.at[pl.ds(pl.multiple_of(me * features, 16), features), :]
+    keep = pltpu.make_async_copy(x_ref, own_block, own_sem.at[0])
+    if reach:
+        start(0, 1, me, False)
+        start(1, 1, me, False)
+    start(0, 0, me, True)
+    keep.start()
+    for distance in range(1, reach + 1):
+        for way in (0, 1):
+            origin = origin_of(way, distance)
+            copy(way, distance, origin, False).wait_recv()
+            if distance < reach:
+                start(way, distance + 1, origin, False)
+            start(way, distance, origin, True)
+    other = 1 - 2 * core
+    copy(0, 0, me + other, True).wait_recv()
+    for distance in range(1, reach + 1):
+        for way in (0, 1):
+            copy(way, distance, origin_of(way, distance) + other, True).wait_recv()
+    keep.wait()
+    for args in sent:
+        copy(*args).wait_send()
+
+
+def gather_rows(x, collective_id):
+    tensors = lax.axis_size("tensor")
+    ring = max(2 * (tensors // 4), 1)
+    vmem = pl.BlockSpec(memory_space=pltpu.VMEM)
+    dma = pltpu.SemaphoreType.DMA
+    return pl.pallas_call(
+        functools.partial(gather_kernel, tensors),
+        out_shape=jax.ShapeDtypeStruct((tensors * x.shape[0], x.shape[1]), x.dtype),
+        in_specs=[vmem],
+        out_specs=vmem,
+        scratch_shapes=[dma((ring,)), dma((ring,)), dma((ring + 1,)), dma((ring + 1,)), dma((1,))],
+        compiler_params=pltpu.CompilerParams(
+            collective_id=collective_id, has_side_effects=True, vmem_limit_bytes=24 * 1024 * 1024
+        ),
+    )(x)
+
+
+def scatter_kernel(tensors, x_ref, out_ref, near, stage, far, send_near, recv_near, send_far, recv_far):
+    me = lax.axis_index("tensor")
+    chips = tensors // 2
+    chip, core = me // 2, me % 2
+    mate = chip * 2 + 1 - core
+    features = out_ref.shape[0]
+
+    barrier = pltpu.get_barrier_semaphore()
+    chips_out = [lax.rem(chip + step, chips) for step in range(1, chips)]
+    greeted = [mate] + [there * 2 + core for there in chips_out]
+    for device in greeted:
+        pl.semaphore_signal(barrier, inc=1, device_id={"tensor": device}, device_id_type=MESH)
+    pl.semaphore_wait(barrier, len(greeted))
+
+    def rows_of(device):
+        return pl.ds(pl.multiple_of(device * features, 16), features)
+
+    def near_copy(there):
+        return pltpu.make_async_remote_copy(
+            src_ref=x_ref.at[rows_of(there * 2 + 1 - core), :], dst_ref=near.at[there],
+            send_sem=send_near.at[there], recv_sem=recv_near.at[there],
+            device_id={"tensor": mate}, device_id_type=MESH,
+        )
+
+    def far_copy(source, there):
+        return pltpu.make_async_remote_copy(
+            src_ref=stage.at[there], dst_ref=far.at[source],
+            send_sem=send_far.at[there], recv_sem=recv_far.at[source],
+            device_id={"tensor": there * 2 + core}, device_id_type=MESH,
+        )
+
+    def pair_sum(there):
+        near_copy(there).wait_recv()
+        mine = x_ref[rows_of(there * 2 + core), :].astype(jnp.float32)
+        return mine + near[there].astype(jnp.float32)
+
+    for there in chips_out + [chip]:
+        near_copy(there).start()
+    for there in chips_out:
+        stage[there] = pair_sum(there).astype(stage.dtype)
+        far_copy(chip, there).start()
+    total = pair_sum(chip)
+    for there in chips_out:
+        far_copy(there, there).wait_recv()
+        total = total + far[there].astype(jnp.float32)
+    out_ref[...] = total.astype(out_ref.dtype)
+    for there in chips_out + [chip]:
+        near_copy(there).wait_send()
+    for there in chips_out:
+        far_copy(chip, there).wait_send()
+
+
+def scatter_rows(x, collective_id):
+    tensors = lax.axis_size("tensor")
+    chips = tensors // 2
+    features = x.shape[0] // tensors
+    vmem = pl.BlockSpec(memory_space=pltpu.VMEM)
+    dma = pltpu.SemaphoreType.DMA
+    held = pltpu.VMEM((chips, features, x.shape[1]), x.dtype)
+    return pl.pallas_call(
+        functools.partial(scatter_kernel, tensors),
+        out_shape=jax.ShapeDtypeStruct((features, x.shape[1]), x.dtype),
+        in_specs=[vmem],
+        out_specs=vmem,
+        scratch_shapes=[held, held, held] + [dma((chips,))] * 4,
+        compiler_params=pltpu.CompilerParams(
+            collective_id=collective_id, has_side_effects=True, vmem_limit_bytes=24 * 1024 * 1024
+        ),
+    )(x)
+
+
+def exchange_kernel(tensors, x_ref, out_ref, held, send, recv):
+    me = lax.axis_index("tensor")
+    barrier = pltpu.get_barrier_semaphore()
+    others = [lax.rem(me + step, tensors) for step in range(1, tensors)]
+    for other in others:
+        pl.semaphore_signal(barrier, inc=1, device_id={"tensor": other}, device_id_type=MESH)
+    pl.semaphore_wait(barrier, tensors - 1)
+
+    def copy(source, other):
+        return pltpu.make_async_remote_copy(
+            src_ref=x_ref, dst_ref=held.at[source], send_sem=send.at[other], recv_sem=recv.at[source],
+            device_id={"tensor": other}, device_id_type=MESH,
+        )
+
+    for other in others:
+        copy(me, other).start()
+    held[me] = x_ref[...]
+    for other in others:
+        copy(other, other).wait_recv()
+    out_ref[...] = jnp.sum(held[...], axis=0)
+    for other in others:
+        copy(me, other).wait_send()
+
+
+def exchange(x, collective_id):
+    tensors = lax.axis_size("tensor")
+    vmem = pl.BlockSpec(memory_space=pltpu.VMEM)
+    dma = pltpu.SemaphoreType.DMA
+    return pl.pallas_call(
+        functools.partial(exchange_kernel, tensors),
+        out_shape=jax.ShapeDtypeStruct(x.shape, x.dtype),
+        in_specs=[vmem],
+        out_specs=vmem,
+        scratch_shapes=[pltpu.VMEM((tensors,) + x.shape, x.dtype), dma((tensors,)), dma((tensors,))],
+        compiler_params=pltpu.CompilerParams(
+            collective_id=collective_id, has_side_effects=True, vmem_limit_bytes=24 * 1024 * 1024
+        ),
+    )(x)
+
+
+def packed_sum(parts, collective_id):
+    flat = jnp.concatenate([jnp.reshape(part, (-1,)) for part in parts])
+    rows = -(-flat.shape[0] // 1024) * 8
+    flat = jnp.pad(flat, (0, rows * 128 - flat.shape[0])).reshape(rows, 128)
+    flat = exchange(flat, collective_id).reshape(-1)
+    sums, start = [], 0
+    for part in parts:
+        sums.append(flat[start : start + part.size].reshape(part.shape))
+        start += part.size
+    return sums
 
 
 def chain(part_grad, part_loss, local_weight):
@@ -197,10 +438,12 @@
             jax.ShapeDtypeStruct((features, rows), jnp.bfloat16),
             jax.ShapeDtypeStruct((width, rows), jnp.bfloat16),
             jax.ShapeDtypeStruct((8, 128), jnp.float32),
+            jax.ShapeDtypeStruct((8, 128), jnp.float32),
         ),
         in_specs=[vmem] * 3,
-        out_specs=(vmem, vmem, vmem),
+        out_specs=(vmem, vmem, vmem, vmem),
         scratch_shapes=[
+            pltpu.VMEM((features, lanes), jnp.float32),
             pltpu.VMEM((max(sections - 1, 1), 8, 128), jnp.float32),
             dma((sections,)),
             dma((sections,)),
@@ -232,38 +475,36 @@
     row_start = section_index * share_rows
     hidden_rows = lax.dynamic_slice_in_dim(hidden_last, row_start, share_rows, 0)
     head_slice = head_weight
-    logits = jnp.dot(
-        lax.all_gather(hidden_rows, "tensor", axis=1, tiled=True),
+    logits = lax.dot_general(
+        gather_rows(hidden_rows.T, 3),
         head_slice,
+        (((0,), (0,)), ((), ())),
         preferred_element_type=jnp.float32,
     )
     exponent = jnp.exp(logits)
     label_hit = (
         lax.dynamic_slice_in_dim(labels, row_start, share_rows, 0)[:, None] == columns[None, :]
     )
-    denominator, picked = lax.psum(
+    denominator, picked = packed_sum(
         (
             jnp.sum(exponent, axis=1),
             jnp.sum(jnp.where(label_hit, logits, jnp.zeros_like(logits)), axis=1),
         ),
-        "tensor",
+        1,
     )
     losses = jnp.log(denominator) - picked
     logit_grad = (
         (exponent / denominator[:, None] - label_hit.astype(jnp.float32)) / all_rows
     ).astype(jnp.bfloat16)
     head_slice = head_weight
-    shares = lax.psum_scatter(
+    part_grad = scatter_rows(
         lax.dot_general(
             head_slice, logit_grad, (((1,), (1,)), ((), ())), preferred_element_type=jnp.float32
-        ),
-        "tensor",
-        scatter_dimension=0,
-        tiled=True,
-    )
-    part_grad = shares.astype(jnp.bfloat16)
+        ).astype(jnp.bfloat16),
+        4,
+    )
     part_loss = jnp.sum(losses)
-    outputs, gathered, total = chain(part_grad, part_loss, local_weight)
+    outputs, gathered, total, weight_squares = chain(part_grad, part_loss, local_weight)
     loss = total[0, 0] / all_rows
     gradient = lax.dot_general(
         saved_all, gathered, (((0,), (1,)), ((), ())), preferred_element_type=jnp.float32
@@ -275,8 +516,8 @@
     row_new = decay_rate * row_state[0] + (1.0 - decay_rate) * jnp.mean(squares, axis=1)
     col_part = jnp.sum(squares, axis=0)
     scaled_part = jnp.sum(square / row_new[:, None], axis=0)
-    col_sum, scaled_sum, row_total, weight_total = lax.psum(
-        (col_part, scaled_part, jnp.sum(row_new), jnp.sum(weight_float * weight_float)), "tensor"
+    col_sum, scaled_sum, row_total, weight_total = packed_sum(
+        (col_part, scaled_part, jnp.sum(row_new), jnp.sum(weight_squares)), 2
     )
     col_new = decay_rate * col_state[0] + (1.0 - decay_rate) * (col_sum / model_width)
     update_total = row_total * jnp.sum(scaled_sum / col_new)

time: 417 us -> 336 us (0.81)
  waiting for transfers between devices: 69.3 us -> 0 us
  Pallas kernels: 182 us -> 230 us
  blocking collectives: 43.7 us -> 0 us
  between operations: 18.7 us -> 5.3 us
    pallas_call x0 -> x4, Pallas kernels: none -> 58.6 us  [the longest x1 21.3 us: gather_rows(): pl.pallas_call(functools.partial(gather_kernel, tensors), out_shape=jax.S...]
    psum x2 -> x0, blocking collectives: 43.7 us -> none  [the longest x1 28.5 us: body(): lax.psum((col_part, scaled_part, jnp.sum(row_new), jnp.sum(weight_float *...]
    reduce_scatter x1 -> x0, waiting for transfers between devices: 40.1 us -> none  [body(): lax.psum_scatter(lax.dot_general(head_slice, logit_grad, (((1,), (1,)), (...]
    all_gather x1 -> x0, waiting for transfers between devices: 29.2 us -> none  [body(): lax.all_gather(hidden_rows, 'tensor', axis=1, tiled=True)]
    pallas_call x1, Pallas kernels: 182 us -> 172 us  [chain(): pl.pallas_call(functools.partial(chain_kernel, sections, tensors), out_sh...]
    reduce_sum x1, other arithmetic: 14.2 us -> 9.72 us  [body(): scaled_part = jnp.sum(square / row_new[:, None], axis=0)]
  transfers between devices with their start and end apart: 2 -> 0, of which waited for: 2 -> 0; matrix products, arithmetic and copies ran while one was open for 0% -> 0% of each run, Pallas kernels for 0% -> 0%
where the time goes in v2:
time: 336 us; the launch traced here: 335 us
  Pallas kernels  230 us (68%)
  matrix products  62.9 us (19%)
  other arithmetic  30.8 us (9%)
  local copies, waits for them, and re-layouts  5.84 us (2%)
  between operations  5.3 us (2%)
    pallas_call x1, Pallas kernels, chain(): pl.pallas_call(functools.partial(chain_kernel, sections, tensors), out_sh...  172 us
    dot_general x1, matrix products, body(): lax.dot_general(head_slice, logit_grad, (((1,), (1,)), ((), ())), preferr...  28.3 us
    dot_general x1, matrix products, body(): lax.dot_general(gather_rows(hidden_rows.T, 3), head_slice, (((0,), (0,)),...  22.1 us
    pallas_call x1, Pallas kernels, gather_rows(): pl.pallas_call(functools.partial(gather_kernel, tensors), out_shape=jax.S...  21.3 us
    pallas_call x1, Pallas kernels, scatter_rows(): pl.pallas_call(functools.partial(scatter_kernel, tensors), out_shape=jax....  20 us
    pallas_call x2, Pallas kernels, exchange(): pl.pallas_call(functools.partial(exchange_kernel, tensors), out_shape=jax...  17.2 us
    broadcast_in_dim x1, other arithmetic, body(): new_weight[None]  15.9 us
    dot_general x1, matrix products, body(): lax.dot_general(saved_all, gathered, (((0,), (1,)), ((), ())), preferred_...  12.5 us

profile of v2, /device:TPU:0, one launch (start us, length us, event | category | flops | bytes accessed | tf_op | source)
XLA Modules:
  0.0 335.0 jit_solution(7677210455320536761)
XLA Ops:
  0.7 0.8 dynamic_slice.7
  1.5 0.7 multiply_reduce_fusion.2
  2.2 0.8 multiply_reduce_fusion.1
  3.0 1.0 dynamic-slice_bitcast_fusion.x_ref
  4.0 21.3 %shard_map.110 = bf16[6656,128]{1,0:T(8,128)(2,1)S(1)} custom-call(bf16[832,128]{1,0:T(8,128)(2,1)S(1)} %dynamic-slice_bitcast_fusion.x_ref), custom_call_target="tpu_custom_call" | custom-call | tf_op jit(solution)/shard_map/pallas_call | solution.py:292
  25.3 22.1 %exponential_reduce_fusion = (f32[128]{0:T(128)S(1)}, f32[128]{0:T(128)S(1)}, f32[128,4000]{0,1:T(8,128)}) fusion(s32[4000]{0:T(1024)S(1)} %iota_add_fusion, s32[128]{0:T(128)S(1)} %dynamic_slice.7, bf16[6656,4000]{0,1:T(8,128)(2,1)} %param.9, bf16[6656,128]{1,0:T(8,128)(2,1)S(1)} %shard_map.110), kind=kOutput, calls=%fused_computation.18 | convolution fusion | flops 6817792000 | bytes 57017472 | tf_op jit(solution)/shard_map/dot_general | solution.py:478
  47.4 5.9 %shard_map.111 = f32[8,128]{1,0:T(8,128)S(1)} custom-call(f32[8,128]{1,0:T(8,128)S(1)} %fusion.22.x_ref), custom_call_target="tpu_custom_call" | custom-call | tf_op jit(solution)/shard_map/pallas_call | solution.py:403
  53.4 0.6 fusion.23
  54.0 28.3 %fusion.7.x_ref = bf16[6656,128]{1,0:T(8,128)(2,1)S(1)} fusion(bf16[6656,4000]{0,1:T(8,128)(2,1)} %param.9, f32[128,4000]{0,1:T(8,128)} %get-tuple-element.26, f32[128]{0:T(128)S(1)} %slice_bitcast_fusion, s32[128]{0:T(128)S(1)} %dynamic_slice.7, s32[4000]{0:T(1024)S(1)} %iota_add_fusion), kind=kOutput, calls=%fused_computation.11 | convolution fusion | flops 6819667968 | bytes 57016960 | tf_op jit(solution)/shard_map/dot_general | solution.py:501
  82.3 20.0 %shard_map.112.part_ref = bf16[832,128]{1,0:T(8,128)(2,1)S(1)} custom-call(bf16[6656,128]{1,0:T(8,128)(2,1)S(1)} %fusion.7.x_ref), custom_call_target="tpu_custom_call" | custom-call | tf_op jit(solution)/shard_map/pallas_call | solution.py:363
  102.3 0.6 broadcast_in_dim.9.loss_ref
  103.0 171.6 %shard_map.113 = (bf16[832,512]{1,0:T(8,128)(2,1)S(1)}, bf16[6656,512]{1,0:T(8,128)(2,1)}, f32[8,128]{1,0:T(8,128)S(1)}, f32[8,128]{1,0:T(8,128)S(1)}) custom-call(bf16[832,128]{1,0:T(8,128)(2,1)S(1)} %shard_map.112.part_ref, f32[8,128]{1,0:T(8,128)S(1)} %broadcast_in_dim.9.loss_ref, bf16[832,6656]{1,0:T(8,128)(2,1)} %bitcast.71), custom_call_target="tpu_custom_call" | custom-call | tf_op jit(solution)/shard_map/pallas_call | solution.py:435
  274.6 0.6 reduce_sum.88
  276.4 12.5 %fusion.4 = (f32[832]{0:T(1024)S(1)}, f32[6656,832]{0,1:T(8,128)}) fusion(bf16[6656,512]{1,0:T(8,128)(2,1)} %get-tuple-element.11, bf16[1,512,832]{1,2,0:T(8,128)(2,1)S(1)} %copy-done), kind=kOutput, calls=%fused_computation.7 | convolution fusion | flops 5687311360 | bytes 29822208 | tf_op jit(solution)/shard_map/dot_general | solution.py:509
  288.9 0.6 reduce_sum.87
  289.5 0.6 reshape_add_fusion
  290.0 9.7 %divide_reduce_fusion = (f32[6656]{0:T(1024)S(1)}, f32[6656]{0:T(1024)S(1)}) fusion(f32[6656,832]{0,1:T(8,128)} %get-tuple-element.28, f32[832]{0:T(1024)S(1)} %get-tuple-element.18), kind=kLoop, calls=%fused_computation.5 | loop fusion | flops 27675648 | bytes 22207744 | tf_op jit(solution)/shard_map/reduce_sum | solution.py:518
  299.8 1.4 concatenate.7
  301.1 11.3 %shard_map.114 = f32[112,128]{1,0:T(8,128)S(1)} custom-call(f32[112,128]{1,0:T(8,128)S(1)} %pad_bitcast_fusion.x_ref), custom_call_target="tpu_custom_call" | custom-call | tf_op jit(solution)/shard_map/pallas_call | solution.py:403
  312.4 0.6 fusion.20
  313.0 0.6 fusion.28
  316.4 0.7 multiply_reduce_fusion
  317.1 15.9 %fusion.6 = bf16[1,832,6656]{2,1,0:T(8,128)(2,1)} fusion(f32[6656,832]{0,1:T(8,128)} %get-tuple-element.28, f32[6656]{0:T(1024)S(1)} %get-tuple-element.19, f32[832]{0:T(1024)S(1)} %get-tuple-element.17, f32[]{:T(128)S(6)} %div.58, bf16[1,832,6656]{2,1,0:T(8,128)(2,1)} %param.11), kind=kLoop, calls=%fused_computation.9 | loop fusion | flops 33226752 | bytes 44332292 | tf_op jit(solution)/shard_map/broadcast_in_dim | solution.py:531
  333.0 0.9 copy.18
  (14 shorter events, 0.6 us)
Async XLA Ops:
  0.6 275.7 %copy-start = (bf16[1,512,832]{1,2,0:T(8,128)(2,1)S(1)}, bf16[1,512,832]{1,2,0:T(8,128)(2,1)}, u32[]{:S(2)}) copy-start(bf16[1,512,832]{1,2,0:T(8,128)(2,1)} %param.10) | copy-start | bytes 2555908
  276.3 13.1 %copy-start.3 = (f32[1,832]{1,0:T(1,128)S(1)}, f32[1,832]{1,0:T(1,128)}, u32[]{:S(2)}) copy-start(f32[1,832]{1,0:T(1,128)} %param.12) | copy-start | bytes 9988
  290.0 26.3 %copy-start.2 = (f32[1,6656]{1,0:T(1,128)S(1)}, f32[1,6656]{1,0:T(1,128)}, u32[]{:S(2)}) copy-start(f32[1,6656]{1,0:T(1,128)} %param.13) | copy-start | bytes 79876
  317.1 16.8 %copy-start.1 = (bf16[1,512,832]{1,2,0:T(8,128)(2,1)S(1)}, bf16[1,512,832]{1,2,0:T(8,128)(2,1)}, u32[]{:S(2)}) copy-start(bf16[1,512,832]{1,2,0:T(8,128)(2,1)} %param.10) | copy-start | bytes 2555908

commit v3 on v2

--- a/solution.py
+++ b/solution.py
@@ -125,7 +125,7 @@
     def _():
         add_squares()
 
-    def advance(share, carry):
+    def begin(share):
         @pl.when((section == last) & (share == last))
         def _():
             own_copy().wait()
@@ -138,8 +138,15 @@
             ring_copy(share, 0, 1, me).start()
             ring_copy(share, 1, 1, me).start()
         mate_copy(share, 0, 0, me).start()
+
+    def advance(share, carry):
         columns = pl.ds(pl.multiple_of(share * lanes, lanes), lanes)
         other = 1 - 2 * core
+
+        def begin_next():
+            @pl.when(share < last)
+            def _():
+                begin(share + 1)
 
         def product_of(owner_chip, first):
             if owner_chip is None:
@@ -167,8 +174,12 @@
                 mate_copy(share, way, distance, origin).start()
             for way in (0, 1):
                 mate_copy(share, way, distance, origin_of(way, distance) + other).wait_recv()
+                if distance == reach and way == 1:
+                    begin_next()
                 if split and (way == 1 or 2 * distance < chips):
                     product_of(origin_of(way, distance) // 2, False)
+        if not reach:
+            begin_next()
         if not split:
             product_of(None, True)
         mine = g_ref[pl.ds(pl.multiple_of(me * features, 16), features), columns]
@@ -180,6 +191,7 @@
 
         return carry
 
+    begin(0)
     lax.fori_loop(0, sections, advance, 0)
 
     @pl.when(section == last)
@@ -334,8 +346,7 @@
 
     def pair_sum(there):
         near_copy(there).wait_recv()
-        mine = x_ref[rows_of(there * 2 + core), :].astype(jnp.float32)
-        return mine + near[there].astype(jnp.float32)
+        return x_ref[rows_of(there * 2 + core), :] + near[there]
 
     for there in chips_out + [chip]:
         near_copy(there).start()
@@ -359,13 +370,13 @@
     features = x.shape[0] // tensors
     vmem = pl.BlockSpec(memory_space=pltpu.VMEM)
     dma = pltpu.SemaphoreType.DMA
-    held = pltpu.VMEM((chips, features, x.shape[1]), x.dtype)
+    held = pltpu.VMEM((chips, features, x.shape[1]), jnp.bfloat16)
     return pl.pallas_call(
         functools.partial(scatter_kernel, tensors),
-        out_shape=jax.ShapeDtypeStruct((features, x.shape[1]), x.dtype),
+        out_shape=jax.ShapeDtypeStruct((features, x.shape[1]), jnp.bfloat16),
         in_specs=[vmem],
         out_specs=vmem,
-        scratch_shapes=[held, held, held] + [dma((chips,))] * 4,
+        scratch_shapes=[pltpu.VMEM((chips, features, x.shape[1]), x.dtype), held, held] + [dma((chips,))] * 4,
         compiler_params=pltpu.CompilerParams(
             collective_id=collective_id, has_side_effects=True, vmem_limit_bytes=24 * 1024 * 1024
         ),
@@ -500,7 +511,7 @@
     part_grad = scatter_rows(
         lax.dot_general(
             head_slice, logit_grad, (((1,), (1,)), ((), ())), preferred_element_type=jnp.float32
-        ).astype(jnp.bfloat16),
+        ),
         4,
     )
     part_loss = jnp.sum(losses)

time: 336 us -> 337 us (level)
    pallas_call x1, Pallas kernels: 172 us -> 168 us  [chain(): pl.pallas_call(functools.partial(chain_kernel, sections, tensors), out_sh...]
where the time goes in v3:
time: 337 us; the launch traced here: 336 us
  Pallas kernels  227 us (67%)
  matrix products  64.5 us (19%)
  other arithmetic  30.8 us (9%)
  local copies, waits for them, and re-layouts  7.8 us (2%)
  between operations  5.29 us (2%)
    pallas_call x1, Pallas kernels, chain(): pl.pallas_call(functools.partial(chain_kernel, sections, tensors), out_sh...  168 us
    dot_general x1, matrix products, body(): lax.dot_general(head_slice, logit_grad, (((1,), (1,)), ((), ())), preferr...  29.9 us
    dot_general x1, matrix products, body(): lax.dot_general(gather_rows(hidden_rows.T, 3), head_slice, (((0,), (0,)),...  22.1 us
    pallas_call x1, Pallas kernels, gather_rows(): pl.pallas_call(functools.partial(gather_kernel, tensors), out_shape=jax.S...  21.3 us
    pallas_call x1, Pallas kernels, scatter_rows(): pl.pallas_call(functools.partial(scatter_kernel, tensors), out_shape=jax....  20.5 us
    pallas_call x2, Pallas kernels, exchange(): pl.pallas_call(functools.partial(exchange_kernel, tensors), out_shape=jax...  17.6 us
    broadcast_in_dim x1, other arithmetic, body(): new_weight[None]  15.9 us
    dot_general x1, matrix products, body(): lax.dot_general(saved_all, gathered, (((0,), (1,)), ((), ())), preferred_...  12.5 us

profile of v3, /device:TPU:0, one launch (start us, length us, event | category | flops | bytes accessed | tf_op | source)
XLA Modules:
  0.0 335.7 jit_solution(18383072654384699664)
XLA Ops:
  0.7 0.8 dynamic_slice.7
  1.5 0.7 multiply_reduce_fusion.2
  2.2 0.8 multiply_reduce_fusion.1
  3.0 1.0 dynamic-slice_bitcast_fusion.x_ref
  4.0 21.3 %shard_map.110 = bf16[6656,128]{1,0:T(8,128)(2,1)S(1)} custom-call(bf16[832,128]{1,0:T(8,128)(2,1)S(1)} %dynamic-slice_bitcast_fusion.x_ref), custom_call_target="tpu_custom_call" | custom-call | tf_op jit(solution)/shard_map/pallas_call | solution.py:304
  25.3 22.1 %exponential_reduce_fusion = (f32[128]{0:T(128)S(1)}, f32[128]{0:T(128)S(1)}, f32[128,4000]{0,1:T(8,128)}) fusion(s32[4000]{0:T(1024)S(1)} %iota_add_fusion, s32[128]{0:T(128)S(1)} %dynamic_slice.7, bf16[6656,4000]{0,1:T(8,128)(2,1)} %param.9, bf16[6656,128]{1,0:T(8,128)(2,1)S(1)} %shard_map.110), kind=kOutput, calls=%fused_computation.17 | convolution fusion | flops 6817792000 | bytes 57017472 | tf_op jit(solution)/shard_map/dot_general | solution.py:489
  47.4 5.9 %shard_map.111 = f32[8,128]{1,0:T(8,128)S(1)} custom-call(f32[8,128]{1,0:T(8,128)S(1)} %fusion.21.x_ref), custom_call_target="tpu_custom_call" | custom-call | tf_op jit(solution)/shard_map/pallas_call | solution.py:414
  53.4 0.6 fusion.22
  54.0 0.6 broadcast_in_dim.9.loss_ref
  54.7 29.9 %convolution_bitcast_fusion.x_ref = f32[6656,128]{1,0:T(8,128)} fusion(bf16[6656,4000]{0,1:T(8,128)(2,1)} %param.9, f32[128,4000]{0,1:T(8,128)} %get-tuple-element.26, f32[128]{0:T(128)S(1)} %slice_bitcast_fusion, s32[128]{0:T(128)S(1)} %dynamic_slice.7, s32[4000]{0:T(1024)S(1)} %iota_add_fusion), kind=kOutput, calls=%fused_computation.10 | convolution fusion | flops 6818816000 | bytes 58720896 | tf_op jit(solution)/shard_map/dot_general | solution.py:512
  84.5 2.0 copy-done.2
  86.5 20.5 %shard_map.112.part_ref = bf16[832,128]{1,0:T(8,128)(2,1)S(1)} custom-call(f32[6656,128]{1,0:T(8,128)S(1)} %copy-done.2), custom_call_target="tpu_custom_call" | custom-call | tf_op jit(solution)/shard_map/pallas_call | solution.py:374
  107.0 168.0 %shard_map.113 = (bf16[832,512]{1,0:T(8,128)(2,1)S(1)}, bf16[6656,512]{1,0:T(8,128)(2,1)}, f32[8,128]{1,0:T(8,128)S(1)}, f32[8,128]{1,0:T(8,128)S(1)}) custom-call(bf16[832,128]{1,0:T(8,128)(2,1)S(1)} %shard_map.112.part_ref, f32[8,128]{1,0:T(8,128)S(1)} %broadcast_in_dim.9.loss_ref, bf16[832,6656]{1,0:T(8,128)(2,1)} %bitcast.71), custom_call_target="tpu_custom_call" | custom-call | tf_op jit(solution)/shard_map/pallas_call | solution.py:446
  274.9 0.6 reduce_sum.88
  276.7 12.5 %fusion.4 = (f32[832]{0:T(1024)S(1)}, f32[6656,832]{0,1:T(8,128)}) fusion(bf16[6656,512]{1,0:T(8,128)(2,1)} %get-tuple-element.11, bf16[1,512,832]{1,2,0:T(8,128)(2,1)S(1)} %copy-done), kind=kOutput, calls=%fused_computation.7 | convolution fusion | flops 5687311360 | bytes 29822208 | tf_op jit(solution)/shard_map/dot_general | solution.py:520
  289.2 0.6 reduce_sum.87
  289.8 0.6 reshape_add_fusion
  290.4 9.7 %divide_reduce_fusion = (f32[6656]{0:T(1024)S(1)}, f32[6656]{0:T(1024)S(1)}) fusion(f32[6656,832]{0,1:T(8,128)} %get-tuple-element.28, f32[832]{0:T(1024)S(1)} %get-tuple-element.18), kind=kLoop, calls=%fused_computation.5 | loop fusion | flops 27675648 | bytes 22207744 | tf_op jit(solution)/shard_map/reduce_sum | solution.py:529
  300.1 1.4 concatenate.7
  301.5 11.6 %shard_map.114 = f32[112,128]{1,0:T(8,128)S(1)} custom-call(f32[112,128]{1,0:T(8,128)S(1)} %pad_bitcast_fusion.x_ref), custom_call_target="tpu_custom_call" | custom-call | tf_op jit(solution)/shard_map/pallas_call | solution.py:414
  313.2 0.6 fusion.19
  317.1 0.7 multiply_reduce_fusion
  317.8 15.9 %fusion.6 = bf16[1,832,6656]{2,1,0:T(8,128)(2,1)} fusion(f32[6656,832]{0,1:T(8,128)} %get-tuple-element.28, f32[6656]{0:T(1024)S(1)} %get-tuple-element.19, f32[832]{0:T(1024)S(1)} %get-tuple-element.17, f32[]{:T(128)S(6)} %div.58, bf16[1,832,6656]{2,1,0:T(8,128)(2,1)} %param.11), kind=kLoop, calls=%fused_computation.9 | loop fusion | flops 33226752 | bytes 44332292 | tf_op jit(solution)/shard_map/broadcast_in_dim | solution.py:542
  333.7 0.9 copy.18
  (16 shorter events, 1.2 us)
Async XLA Ops:
  0.6 276.1 %copy-start = (bf16[1,512,832]{1,2,0:T(8,128)(2,1)S(1)}, bf16[1,512,832]{1,2,0:T(8,128)(2,1)}, u32[]{:S(2)}) copy-start(bf16[1,512,832]{1,2,0:T(8,128)(2,1)} %param.10) | copy-start | bytes 2555908
  84.5 2.0 copy-start.2
  276.7 13.1 %copy-start.4 = (f32[1,832]{1,0:T(1,128)S(1)}, f32[1,832]{1,0:T(1,128)}, u32[]{:S(2)}) copy-start(f32[1,832]{1,0:T(1,128)} %param.12) | copy-start | bytes 9988
  290.4 26.7 %copy-start.3 = (f32[1,6656]{1,0:T(1,128)S(1)}, f32[1,6656]{1,0:T(1,128)}, u32[]{:S(2)}) copy-start(f32[1,6656]{1,0:T(1,128)} %param.13) | copy-start | bytes 79876
  317.8 16.8 %copy-start.1 = (bf16[1,512,832]{1,2,0:T(8,128)(2,1)S(1)}, bf16[1,512,832]{1,2,0:T(8,128)(2,1)}, u32[]{:S(2)}) copy-start(bf16[1,512,832]{1,2,0:T(8,128)(2,1)} %param.10) | copy-start | bytes 2555908
